TPU v7x, 32 devices: a whole 2x2x4 slice. The times are simulated.
32 devices in a mesh: row: 16 (over z, y, x), col: 2 (over core).
Axes of the slice: x: 2, y: 2, z: 4, core: 2. Of those that a mesh axis runs over, the one named last changes fastest.
Arguments:
- kernel: float32 [1024, 65536], P('row', 'col'), may hold values from -6 to 6
- basis: float32 [65536, 128], P('col', 'row'), may hold values from -0.0234375 to 0.0234375
- responses: float32 [1024, 512], P('row', 'col'), may hold values from -6 to 6
Outputs:
- scores: float32 [1024, 128], P('row')
- loadings: float32 [128, 65536], P('row', 'col')
- weights: float32 [512, 128], P('col')
- deflated: float32 [1024, 65536], P('row', 'col')
- basis_next: float32 [1024, 128], P('row')
All inputs are finite; a program needn't handle non-finite values.
Results may differ from a plain program's by a relative error of at most 0.00012.
Values sent between devices are 32-bit elements; how exact they have to be, the bound alone decides.
A program may use at most 64 MiB of HBM per device.

v0:
```python
import math

import jax
import jax.numpy as jnp
from jax import lax
from jax.sharding import PartitionSpec as P


def local(kernel, basis, responses):
    highest = lax.Precision.HIGHEST
    row_count = kernel.shape[0] * lax.axis_size("row")
    resp_count = responses.shape[1] * lax.axis_size("col")
    root_rows = math.sqrt(row_count)
    partial_proj = jnp.dot(
        kernel, lax.all_gather(basis, "row", axis=1, tiled=True), precision=highest
    )
    projected = lax.psum(partial_proj, "col")
    gram_part = jnp.dot(projected.T, projected, precision=highest) / row_count
    cross_part = jnp.dot(responses.T, projected, precision=highest)
    gram_mat, cross = lax.psum((gram_part, cross_part), "row")
    factor = jnp.linalg.cholesky(gram_mat)
    scores = jax.scipy.linalg.solve_triangular(factor, projected.T, lower=True).T
    weights = jax.scipy.linalg.solve_triangular(factor, cross.T, lower=True).T / root_rows
    next_part = jnp.dot(responses, weights, precision=highest) / math.sqrt(resp_count)
    basis_next = lax.psum(next_part, "col")
    loadings = lax.psum_scatter(
        jnp.dot(scores.T, kernel, precision=highest) / root_rows,
        "row",
        scatter_dimension=0,
        tiled=True,
    )
    all_loadings = lax.all_gather(loadings, "row", axis=0, tiled=True)
    deflated = kernel - jnp.dot(scores, all_loadings, precision=highest) / root_rows
    return (scores, loadings, weights, deflated, basis_next)


def solution(mesh):
    return jax.shard_map(
        local,
        mesh=mesh,
        in_specs=(P("row", "col"), P("col", "row"), P("row", "col")),
        out_specs=(
            P("row", None),
            P("row", "col"),
            P("col", None),
            P("row", "col"),
            P("row", None),
        ),
        check_vma=False,
    )
```

profile of v0, /device:TPU:0, one launch (start us, length us, event | category | flops | bytes accessed | tf_op | source)
XLA Modules:
  0.0 949.3 jit_solution(3972383081146819063)
XLA Ops:
  7.2 0.0 copy-start
  7.2 0.0 all-gather.3.cloned.1.call-start
  7.2 0.7 all-gather.3.cloned.1.call-update
  7.9 0.0 all-reduce.3.cloned.1.call-start
  8.0 196.6 %all-gather.3.cloned.1.call-done = f32[32768,128]{0,1:T(8,128)} async-done(((f32[32768,8]{0,1:T(8,128)}), f32[32768,128]{0,1:T(8,128)}) %all-gather.3.cloned.1.call-update) | async-done | bytes 16777232 | tf_op jit(solution)/shard_map/all_gather | solution.py:15
  204.5 21.3 %fusion.7 = f32[64,128]{1,0:T(8,128)S(1)} fusion(f32[64,32768]{1,0:T(8,128)} %param.3, f32[32768,128]{0,1:T(8,128)} %all-gather.3.cloned.1.call-done), kind=kOutput, calls=%fused_computation.19 | convolution fusion | flops 3221225472 | bytes 25198592 | tf_op jit(solution)/shard_map/dot_general | solution.py:14
  225.8 3.4 psum.28
  229.3 0.9 convolution_multiply_fusion.3
  230.2 1.0 convolution_bitcast_fusion
  231.2 0.0 all-reduce.3.cloned.1.call-update
  231.2 0.2 reduce-scatter.2.cloned.1.call-start
  231.4 106.2 %all-reduce.3.cloned.1.call-done = (f32[128,128]{0,1:T(8,128)}, f32[256,128]{0,1:T(8,128)}) async-done(((f32[128,128]{0,1:T(8,128)}, f32[256,128]{0,1:T(8,128)}), (f32[128,128]{0,1:T(8,128)}, f32[256,128]{0,1:T(8,128)})) %all-reduce.3.cloned.1.call-update) | async-done | bytes 196624 | tf_op jit(solution)/shard_map/psum | solution.py:20
  337.6 0.9 copy.9
  338.6 0.9 fusion.6
  339.4 11.7 %cholesky.16 = f32[128,128]{1,0:T(8,128)S(1)} custom-call(f32[128,128]{1,0:T(8,128)S(1)} %fusion.6), custom_call_target="Cholesky" | custom-call | tf_op jit(solution)/shard_map/jit(cholesky)/cholesky | solution.py:21
  351.2 0.6 compare_reduce_fusion
  351.8 0.7 fusion.2
  352.5 9.8 %custom-call.10 = f32[1,128,128]{1,2,0:T(8,128)S(1)} custom-call(f32[1,128,128]{2,1,0:T(8,128)S(1)} %fusion.2), custom_call_target="InvertDiagBlocksLowerTriangular" | custom-call | tf_op jit(solution)/shard_map/jit(_solve_triangular)/triangular_solve | solution.py:22
  362.3 0.2 fusion.4
  362.5 0.0 copy-start.2
  362.5 18.0 %convolution_multiply_fusion = f32[128,32768]{1,0:T(8,128)} fusion(f32[128,64]{0,1:T(8,128)S(1)} %fusion.4, f32[64,32768]{1,0:T(8,128)} %param.3), kind=kOutput, calls=%fused_computation | convolution fusion | flops 3225419776 | bytes 25198592 | tf_op jit(solution)/shard_map/dot_general | solution.py:27
  380.5 0.0 reduce-scatter.2.cloned.1.call-update
  380.5 0.0 all-gather.5.cloned.1.call-start
  380.6 345.6 %reduce-scatter.2.cloned.1.call-done = f32[8,32768]{1,0:T(8,128)} async-done(((f32[128,32768]{1,0:T(8,128)}), f32[8,32768]{1,0:T(8,128)}) %reduce-scatter.2.cloned.1.call-update) | async-done | bytes 1048592 | tf_op jit(solution)/shard_map/reduce_scatter | solution.py:26
  726.1 0.0 all-gather.5.cloned.1.call-update
  726.2 0.0 copy-done.3
  726.2 0.4 convolution_multiply_fusion.2
  726.6 0.0 copy-start.1
  726.6 0.2 fusion.1
  726.8 4.1 psum.31
  730.9 195.1 %all-gather.5.cloned.1.call-done = f32[128,32768]{1,0:T(8,128)} async-done(((f32[8,32768]{1,0:T(8,128)}), f32[128,32768]{1,0:T(8,128)}) %all-gather.5.cloned.1.call-update) | async-done | bytes 16777232 | tf_op jit(solution)/shard_map/all_gather | solution.py:32
  926.0 16.7 %fusion = f32[64,32768]{1,0:T(8,128)} fusion(f32[64,32768]{1,0:T(8,128)} %param.3, f32[128,64]{0,1:T(8,128)S(1)} %fusion.4, f32[128,32768]{1,0:T(8,128)} %all-gather.5.cloned.1.call-done), kind=kOutput, calls=%fused_computation.2 | convolution fusion | flops 3225419776 | bytes 33587200 | tf_op jit(solution)/shard_map/dot_general | solution.py:33
  (5 shorter events, 0.0 us)
Async XLA Ops:
  7.2 223.0 %copy-start = (f32[64,256]{1,0:T(8,128)S(1)}, f32[64,256]{1,0:T(8,128)}, u32[]{:S(2)}) copy-start(f32[64,256]{1,0:T(8,128)} %param.5) | copy-start | bytes 196612
  7.2 197.3 %all-gather.3.cloned.1.call-start = ((), (), s32[]{:S(2)}) async-start(), calls=%async_computation.1 | async-start | bytes 17825792 | tf_op jit(solution)/shard_map/all_gather | solution.py:15
  7.9 329.7 %all-reduce.3.cloned.1.call-start = ((), (), s32[]{:S(2)}) async-start(), calls=%async_computation.4 | async-start | bytes 393216 | tf_op jit(solution)/shard_map/psum | solution.py:20
  231.2 495.0 %reduce-scatter.2.cloned.1.call-start = ((), (), s32[]{:S(2)}) async-start(), calls=%async_computation.2 | async-start | bytes 17825792 | tf_op jit(solution)/shard_map/reduce_scatter | solution.py:26
  362.5 563.5 %copy-start.2 = (f32[128,64]{0,1:T(8,128)}, f32[128,64]{0,1:T(8,128)S(1)}, u32[]{:S(2)}) copy-start(f32[128,64]{0,1:T(8,128)S(1)} %fusion.4) | copy-start | bytes 98308
  380.5 345.7 %copy-start.3 = (f32[256,128]{0,1:T(8,128)S(1)}, f32[256,128]{0,1:T(8,128)}, u32[]{:S(2)}) copy-start(f32[256,128]{0,1:T(8,128)} %get-tuple-element.6) | copy-start | bytes 393220
  380.5 545.5 %all-gather.5.cloned.1.call-start = ((), (), s32[]{:S(2)}) async-start(), calls=%async_computation.3 | async-start | bytes 17825792 | tf_op jit(solution)/shard_map/all_gather | solution.py:32
  726.6 216.2 %copy-start.1 = (f32[256,128]{1,0:T(8,128)}, f32[256,128]{1,0:T(8,128)S(1)}, u32[]{:S(2)}) copy-start(f32[256,128]{1,0:T(8,128)S(1)} %convolution_multiply_fusion.2) | copy-start | bytes 393220
Sparse Core Ops, SparseCore 0:
  10.8 193.7 all-gather.2
  231.3 106.2 all-reduce.2
  380.7 345.4 reduce-scatter.1
  729.3 196.6 all-gather.4
where the time goes:
time: 950 us; the launch traced here: 949 us
  waiting for transfers between devices  844 us (89%)
  matrix products  58.7 us (6%)
  other arithmetic  23.7 us (2%)
  between operations  13.9 us (1%)
    reduce_scatter x1, waiting for transfers between devices, local(): lax.psum_scatter(jnp.dot(scores.T, kernel, precision=highest) / root_rows...  346 us
    all_gather x1, waiting for transfers between devices, local(): lax.all_gather(basis, 'row', axis=1, tiled=True)  197 us
    all_gather x1, waiting for transfers between devices, local(): all_loadings = lax.all_gather(loadings, 'row', axis=0, tiled=True)  195 us
    psum x1, waiting for transfers between devices, local(): gram_mat, cross = lax.psum((gram_part, cross_part), 'row')  106 us
    dot_general x1, matrix products, local(): jnp.dot(kernel, lax.all_gather(basis, 'row', axis=1, tiled=True), precisi...  21.3 us
  transfers between devices with their start and end apart: 4, of which 4 were waited for; matrix products, arithmetic and copies ran while one was open for 0% of the time, Pallas kernels for 0%

commit v1 on v0

v1 whole, which is shorter than its diff:
```python
import math

import jax
import jax.numpy as jnp
from jax import lax
from jax.experimental import pallas as pl
from jax.experimental.pallas import tpu as pltpu
from jax.sharding import PartitionSpec as P

MESH = pl.DeviceIdType.MESH
BACK = {"x": "x", "y": "y", "up": "down", "down": "up"}


def when(conds):
    conds = [c for c in conds if c is not None]
    if not conds:
        return lambda f: f()
    both = conds[0]
    for c in conds[1:]:
        both = jnp.logical_and(both, c)
    return pl.when(both)


class Grid:
    def __init__(self, n):
        self.n = n
        self.size = {"z": n // 4, "y": 2, "x": 2} if n % 4 == 0 else {"z": n, "y": 1, "x": 1}
        z = self.size["z"]
        self.rels = [
            (dz, fy, fx)
            for dz in range(1 - z, z)
            for fy in range(self.size["y"])
            for fx in range(self.size["x"])
        ]
        self.rels.sort(key=lambda r: (abs(r[0]) + r[1] + r[2], -abs(r[0])))

    def locate(self):
        me = lax.axis_index("row")
        ny, nx = self.size["y"], self.size["x"]
        self.me = me
        self.z = me // (ny * nx)
        self.y = (me // nx) % ny
        self.x = me % nx

    def coords(self, rel):
        dz, fy, fx = rel
        return {
            "z": self.z + dz,
            "y": 1 - self.y if fy else self.y,
            "x": 1 - self.x if fx else self.x,
        }

    def index(self, rel):
        c = self.coords(rel)
        return (c["z"] * self.size["y"] + c["y"]) * self.size["x"] + c["x"]

    def valid(self, rel):
        dz = rel[0]
        if dz == 0:
            return None
        return self.z < self.size["z"] - dz if dz > 0 else self.z >= -dz

    def neighbour(self, link):
        rel = {"x": (0, 0, 1), "y": (0, 1, 0), "up": (1, 0, 0), "down": (-1, 0, 0)}[link]
        return self.index(rel)

    def has(self, link):
        if link == "up":
            return self.z < self.size["z"] - 1
        if link == "down":
            return self.z > 0
        return None

    def links(self):
        found = [d for d in "xy" if self.size[d] > 1]
        return found + (["up", "down"] if self.size["z"] > 1 else [])

    def last(self, order, rel):
        differs = {"z": rel[0] != 0, "y": rel[1] != 0, "x": rel[2] != 0}
        found = [k for k, d in enumerate(order) if differs[d]]
        return found[-1] if found else -1

    def away(self, order, rel):
        k = self.last(order, rel)
        found = []
        for j, d in enumerate(order):
            if j < k or self.size[d] == 1:
                continue
            if d != "z":
                found += [d] if j > k else []
            elif j > k:
                found += ["up", "down"]
            else:
                found += ["down" if rel[0] > 0 else "up"]
        return found

    def towards(self, order, rel):
        d = order[self.last(order, rel)]
        if d != "z":
            return d
        return "up" if rel[0] > 0 else "down"

    def slot_dims(self, order, link):
        if link in "xy":
            return order[: order.index(link)]
        return order[: order.index("z") + 1]

    def slots(self, order, link):
        return math.prod(self.size[d] for d in self.slot_dims(order, link))

    def slot(self, order, link, rel):
        c = self.coords(rel)
        at = 0
        for d in self.slot_dims(order, link):
            at = at * self.size[d] + c[d]
        return at

    def barrier(self):
        barrier = pltpu.get_barrier_semaphore()
        count = 0
        for link in self.links():
            cond = self.has(link)

            @when([cond])
            def _(link=link):
                pl.semaphore_signal(
                    barrier, inc=1, device_id={"row": self.neighbour(link)}, device_id_type=MESH
                )

            count = count + (1 if cond is None else cond.astype(jnp.int32))
        pl.semaphore_wait(barrier, count)


def parts_of(width):
    tile = 128
    tiles = width // tile
    thin = tiles // 9
    if thin == 0:
        return [(0, width, "zyx")]
    wide = [(tiles - 2 * thin + 3 - i) // 4 for i in range(4)]
    pieces = [
        (wide[0], "zyx"),
        (wide[1], "zxy"),
        (thin, "xyz"),
        (thin, "yxz"),
        (wide[2], "zyx"),
        (wide[3], "zxy"),
    ]
    found, start = [], 0
    for count, order in pieces:
        if count:
            found.append((start * tile, count * tile, order))
            start += count
    return found


def sem_shapes(grid, orders):
    return [
        [pltpu.SemaphoreType.DMA((grid.slots(order, link),)) for link in grid.links()]
        for order in orders
    ]


def gather_start(grid, rel, part, order, src, dst, send, recv):
    row = grid.index(rel)
    for link in grid.away(order, rel):

        @when([grid.valid(rel), grid.has(link)])
        def _(link=link):
            gather_copy(grid, rel, part, order, link, src(row), dst(row), send, recv).start()


def gather_copy(grid, rel, part, order, link, src, dst, send, recv):
    return pltpu.make_async_remote_copy(
        src_ref=src,
        dst_ref=dst,
        send_sem=send[part][grid.links().index(link)].at[grid.slot(order, link, rel)],
        recv_sem=recv.at[part, grid.index(rel)],
        device_id={"row": grid.neighbour(link)},
        device_id_type=MESH,
    )


def gather_finish(grid, parts, dst, send, recv):
    for rel in grid.rels[1:]:
        for part, order in parts:

            @when([grid.valid(rel)])
            def _(rel=rel, part=part, order=order):
                row = grid.index(rel)
                pltpu.make_async_copy(dst(part, row), dst(part, row), recv.at[part, row]).wait()

            gather_start(
                grid, rel, part, order, lambda r: dst(part, r), lambda r: dst(part, r), send, recv
            )
    for rel in grid.rels:
        for part, order in parts:
            for link in grid.away(order, rel):

                @when([grid.valid(rel), grid.has(link)])
                def _(rel=rel, part=part, order=order, link=link):
                    ref = dst(part, grid.index(rel))
                    gather_copy(grid, rel, part, order, link, ref, ref, send, recv).wait_send()


def all_gather(block, collective_id):
    n = lax.axis_size("row")
    grid = Grid(n)
    parts = parts_of(block.shape[1]) if block.shape[1] >= 1152 else [(0, block.shape[1], "zyx")]
    numbered = [(i, order) for i, (_, _, order) in enumerate(parts)]

    def kernel(own, out, own_sem, recv, send):
        grid.locate()
        keep = pltpu.make_async_copy(own, out.at[grid.me], own_sem)
        keep.start()
        grid.barrier()

        def dst(part, row):
            start, width, _ = parts[part]
            return out.at[row, :, pl.ds(start, width)]

        for part, order in numbered:
            start, width, _ = parts[part]
            gather_start(
                grid,
                (0, 0, 0),
                part,
                order,
                lambda r: own.at[:, pl.ds(start, width)],
                lambda r: dst(part, r),
                send,
                recv,
            )
        gather_finish(grid, numbered, dst, send, recv)
        keep.wait()

    return pl.pallas_call(
        kernel,
        out_shape=jax.ShapeDtypeStruct((n, *block.shape), block.dtype),
        in_specs=[pl.BlockSpec(memory_space=pl.ANY)],
        out_specs=pl.BlockSpec(memory_space=pl.ANY),
        scratch_shapes=[
            pltpu.SemaphoreType.DMA,
            pltpu.SemaphoreType.DMA((len(parts), n)),
            sem_shapes(grid, [o for _, _, o in parts]),
        ],
        compiler_params=pltpu.CompilerParams(collective_id=collective_id, has_side_effects=True),
    )(block)


def all_reduce(arrays, collective_id):
    n = lax.axis_size("row")
    grid = Grid(n)
    parts = [(i, *p) for i, a in enumerate(arrays) for p in parts_of(a.shape[2])]
    parts.sort(key=lambda p: -p[0])
    orders = [p[3] for p in parts]
    numbered = list(enumerate(orders))
    count = len(arrays)

    def kernel(*refs):
        sources, outs, held = refs[:count], refs[count : 2 * count], refs[2 * count : 3 * count]
        inbox, load_sem, keep_sem, sum_send, sum_recv, send, recv = refs[3 * count :]
        grid.locate()

        def load(i, row):
            return pltpu.make_async_copy(sources[i].at[row], held[i].at[row], load_sem.at[i, row])

        for rel in reversed(grid.rels):
            for i in range(count):

                @when([grid.valid(rel)])
                def _(rel=rel, i=i):
                    load(i, grid.index(rel)).start()

        grid.barrier()

        def kept(part, row):
            i, start, width, _ = parts[part]
            return held[i].at[row, :, pl.ds(start, width)]

        def dst(part, row):
            i, start, width, _ = parts[part]
            return outs[i].at[row, :, pl.ds(start, width)]

        def sum_copy(rel, part, order):
            link = grid.towards(order, rel)
            at = grid.slot(order, BACK[link], rel)
            there = grid.links().index(BACK[link])
            row = grid.index(rel)
            return pltpu.make_async_remote_copy(
                src_ref=kept(part, row),
                dst_ref=inbox[part][there].at[at],
                send_sem=sum_send.at[part, row],
                recv_sem=sum_recv[part][there].at[at],
                device_id={"row": grid.neighbour(link)},
                device_id_type=MESH,
            )

        for rel in reversed(grid.rels):
            for i in range(count):

                @when([grid.valid(rel)])
                def _(rel=rel, i=i):
                    load(i, grid.index(rel)).wait()

            for part, order in numbered:
                i, start, width, _ = parts[part]
                for link in grid.away(order, rel):

                    @when([grid.valid(rel), grid.has(link)])
                    def _(rel=rel, part=part, order=order, link=link):
                        row, at = grid.index(rel), grid.slot(order, link, rel)
                        here = grid.links().index(link)
                        slot = inbox[part][here].at[at]
                        pltpu.make_async_copy(slot, slot, sum_recv[part][here].at[at]).wait()
                        columns = pl.ds(start, width)
                        held[i][row, :, columns] = held[i][row, :, columns] + inbox[part][here][at]

                if rel != (0, 0, 0):

                    @when([grid.valid(rel)])
                    def _(rel=rel, part=part, order=order):
                        sum_copy(rel, part, order).start()

                else:
                    pltpu.make_async_copy(
                        kept(part, grid.me), dst(part, grid.me), keep_sem.at[part]
                    ).start()
                    gather_start(
                        grid,
                        rel,
                        part,
                        order,
                        lambda r: kept(part, r),
                        lambda r: dst(part, r),
                        send,
                        recv,
                    )
        gather_finish(grid, numbered, dst, send, recv)
        for rel in grid.rels:
            for part, order in numbered:
                if rel != (0, 0, 0):

                    @when([grid.valid(rel)])
                    def _(rel=rel, part=part, order=order):
                        sum_copy(rel, part, order).wait_send()

                else:
                    pltpu.make_async_copy(
                        kept(part, grid.me), dst(part, grid.me), keep_sem.at[part]
                    ).wait()

    return pl.pallas_call(
        kernel,
        out_shape=[jax.ShapeDtypeStruct(a.shape, a.dtype) for a in arrays],
        in_specs=[pl.BlockSpec(memory_space=pl.ANY)] * count,
        out_specs=[pl.BlockSpec(memory_space=pl.ANY)] * count,
        scratch_shapes=[
            *[pltpu.VMEM(a.shape, a.dtype) for a in arrays],
            [
                [
                    pltpu.VMEM((grid.slots(order, link), arrays[i].shape[1], width), jnp.float32)
                    for link in grid.links()
                ]
                for i, _, width, order in parts
            ],
            pltpu.SemaphoreType.DMA((count, n)),
            pltpu.SemaphoreType.DMA((len(parts),)),
            pltpu.SemaphoreType.DMA((len(parts), n)),
            sem_shapes(grid, orders),
            sem_shapes(grid, orders),
            pltpu.SemaphoreType.DMA((len(parts), n)),
        ],
        compiler_params=pltpu.CompilerParams(
            collective_id=collective_id, has_side_effects=True, vmem_limit_bytes=60 * 2**20
        ),
    )(*arrays)


def local(kernel, basis, responses):
    highest = lax.Precision.HIGHEST
    n = lax.axis_size("row")
    row_count = kernel.shape[0] * n
    resp_count = responses.shape[1] * lax.axis_size("col")
    comp = basis.shape[1] * n
    root_rows = math.sqrt(row_count)
    last_dims = (((1,), (1,)), ((), ()))
    first_dims = (((0,), (0,)), ((), ()))

    all_basis = all_gather(basis.T, 0).reshape(comp, basis.shape[0])
    partial_proj = lax.dot_general(kernel, all_basis, last_dims, precision=highest)
    projected = lax.psum(partial_proj, "col")
    all_projected = all_gather(projected, 1).reshape(row_count, comp)
    gram_mat = lax.dot_general(all_projected, all_projected, first_dims, precision=highest)
    factor = jnp.linalg.cholesky(gram_mat / row_count)
    scores = jax.scipy.linalg.solve_triangular(factor, projected.T, lower=True).T

    load_part = lax.dot_general(scores, kernel, first_dims, precision=highest) / root_rows
    weight_part = lax.dot_general(responses, scores, first_dims, precision=highest) / root_rows
    all_loadings, all_weights = all_reduce(
        [
            load_part.reshape(n, comp // n, kernel.shape[1]),
            weight_part.reshape(n, responses.shape[1] // n, comp),
        ],
        2,
    )
    loadings = lax.dynamic_index_in_dim(all_loadings, lax.axis_index("row"), keepdims=False)
    weights = all_weights.reshape(responses.shape[1], comp)
    next_part = jnp.dot(responses, weights, precision=highest) / math.sqrt(resp_count)
    basis_next = lax.psum(next_part, "col")
    all_loadings = all_loadings.reshape(comp, kernel.shape[1])
    deflated = kernel - jnp.dot(scores, all_loadings, precision=highest) / root_rows
    return (scores, loadings, weights, deflated, basis_next)


def solution(mesh):
    return jax.shard_map(
        local,
        mesh=mesh,
        in_specs=(P("row", "col"), P("col", "row"), P("row", "col")),
        out_specs=(
            P("row", None),
            P("row", "col"),
            P("col", None),
            P("row", "col"),
            P("row", None),
        ),
        check_vma=False,
    )
```

time: 950 us -> 476 us (0.50)
  waiting for transfers between devices: 844 us -> 0 us
  Pallas kernels: 0 us -> 380 us
  between operations: 13.9 us -> 0.76 us
    all_gather x2 -> x0, waiting for transfers between devices: 392 us -> none  [the longest x1 197 us: local(): lax.all_gather(basis, 'row', axis=1, tiled=True)]
    pallas_call x0 -> x3, Pallas kernels: none -> 380 us  [the longest x1 239 us: all_reduce(): pl.pallas_call(kernel, out_shape=[jax.ShapeDtypeStruct(a.shape, a.dtype)...]
    reduce_scatter x1 -> x0, waiting for transfers between devices: 346 us -> none  [local(): lax.psum_scatter(jnp.dot(scores.T, kernel, precision=highest) / root_rows...]
    psum x1 -> x0, waiting for transfers between devices: 106 us -> none  [local(): gram_mat, cross = lax.psum((gram_part, cross_part), 'row')]
  transfers between devices with their start and end apart: 4 -> 0, of which waited for: 4 -> 0; matrix products, arithmetic and copies ran while one was open for 0% -> 0% of each run, Pallas kernels for 0% -> 0%
where the time goes in v1:
time: 476 us
  Pallas kernels  380 us (80%)
  matrix products  60 us (13%)
  other arithmetic  22.9 us (5%)
  blocking collectives  8 us (2%)
    pallas_call x1, Pallas kernels, all_reduce(): pl.pallas_call(kernel, out_shape=[jax.ShapeDtypeStruct(a.shape, a.dtype)...  239 us
    pallas_call x2, Pallas kernels, all_gather(): pl.pallas_call(kernel, out_shape=jax.ShapeDtypeStruct((n, *block.shape),...  142 us
    dot_general x1, matrix products, local(): lax.dot_general(kernel, all_basis, last_dims, precision=highest)  21.3 us
    dot_general x1, matrix products, local(): lax.dot_general(scores, kernel, first_dims, precision=highest) / root_rows  18.2 us
    dot_general x1, matrix products, local(): jnp.dot(scores, all_loadings, precision=highest) / root_rows  16.8 us
    another operation x3, other arithmetic, local(): factor = jnp.linalg.cholesky(gram_mat / row_count)  12.4 us
    another operation x2, other arithmetic, local(): jax.scipy.linalg.solve_triangular(factor, projected.T, lower=True)  10.5 us

profile of v1, /device:TPU:0, one launch (start us, length us, event | category | flops | bytes accessed | tf_op | source)
XLA Modules:
  0.0 475.7 jit_solution(9804847672750600587)
XLA Ops:
  0.6 0.0 copy-start
  0.6 123.2 %shard_map.74 = f32[16,8,32768]{2,1,0:T(8,128)} custom-call(f32[8,32768]{1,0:T(8,128)} %bitcast.40), custom_call_target="tpu_custom_call" | custom-call | tf_op jit(solution)/shard_map/pallas_call | solution.py:237
  123.8 21.3 %fusion.3 = f32[64,128]{1,0:T(8,128)S(1)} fusion(f32[64,32768]{1,0:T(8,128)} %param.3, f32[16,8,32768]{2,1,0:T(8,128)} %shard_map.74), kind=kOutput, calls=%fused_computation.5 | convolution fusion | flops 3221225472 | bytes 25198592 | tf_op jit(solution)/shard_map/dot_general | solution.py:391
  145.2 4.0 psum.14.own
  149.2 18.6 %shard_map.75 = f32[16,64,128]{2,1,0:T(8,128)} custom-call(f32[64,128]{1,0:T(8,128)} %psum.14.own), custom_call_target="tpu_custom_call" | custom-call | tf_op jit(solution)/shard_map/pallas_call | solution.py:237
  167.7 2.2 convolution_bitcast_fusion
  169.9 0.1 copy.8
  170.0 11.7 %cholesky.16 = f32[128,128]{1,0:T(8,128)S(1)} custom-call(f32[128,128]{1,0:T(8,128)S(1)} %fusion.10), custom_call_target="Cholesky" | custom-call | tf_op jit(solution)/shard_map/jit(cholesky)/cholesky | solution.py:395
  181.8 0.6 compare_reduce_fusion
  182.4 0.7 fusion.7
  183.1 9.8 %custom-call.7 = f32[1,128,128]{1,2,0:T(8,128)S(1)} custom-call(f32[1,128,128]{2,1,0:T(8,128)S(1)} %fusion.7), custom_call_target="InvertDiagBlocksLowerTriangular" | custom-call | tf_op jit(solution)/shard_map/jit(_solve_triangular)/triangular_solve | solution.py:396
  192.9 0.9 fusion.8
  193.8 0.0 copy-start.1
  193.9 18.2 %fusion.refs_0_ = f32[16,8,32768]{2,1,0:T(8,128)} fusion(f32[128,64]{0,1:T(8,128)S(1)} %fusion.8, f32[64,32768]{1,0:T(8,128)} %param.3), kind=kOutput, calls=%fused_computation.1 | convolution fusion | flops 3225419776 | bytes 25198592 | tf_op jit(solution)/shard_map/dot_general | solution.py:398
  212.1 0.0 copy-done
  212.1 0.3 fusion.5
  212.4 0.8 copy.9
  213.2 238.6 %shard_map.76 = (f32[16,8,32768]{2,1,0:T(8,128)}, f32[16,16,128]{2,1,0:T(8,128)}) custom-call(f32[16,8,32768]{2,1,0:T(8,128)} %fusion.refs_0_, f32[16,16,128]{2,1,0:T(8,128)} %bitcast.41), custom_call_target="tpu_custom_call" | custom-call | tf_op jit(solution)/shard_map/pallas_call | solution.py:353
  451.8 0.0 copy-done.1
  451.8 0.0 copy-start.2
  451.8 16.8 %fusion.1 = f32[64,32768]{1,0:T(8,128)} fusion(f32[64,32768]{1,0:T(8,128)} %param.3, f32[128,64]{0,1:T(8,128)S(1)} %fusion.8, f32[16,8,32768]{2,1,0:T(8,128)} %get-tuple-element.7), kind=kOutput, calls=%fused_computation.3 | convolution fusion | flops 3225419776 | bytes 33587200 | tf_op jit(solution)/shard_map/dot_general | solution.py:412
  468.6 2.3 dynamic-slice_bitcast_fusion
  470.9 0.0 copy-done.2
  470.9 0.2 fusion.6
  471.1 4.0 psum.15
  475.1 0.7 copy.11
  (2 shorter events, 0.0 us)
Async XLA Ops:
  0.6 211.5 %copy-start = (f32[64,256]{1,0:T(8,128)S(1)}, f32[64,256]{1,0:T(8,128)}, u32[]{:S(2)}) copy-start(f32[64,256]{1,0:T(8,128)} %param.5) | copy-start | bytes 196612
  193.8 257.9 %copy-start.1 = (f32[128,64]{0,1:T(8,128)}, f32[128,64]{0,1:T(8,128)S(1)}, u32[]{:S(2)}) copy-start(f32[128,64]{0,1:T(8,128)S(1)} %fusion.8) | copy-start | bytes 98308
  451.8 19.1 %copy-start.2 = (f32[16,16,128]{2,1,0:T(8,128)S(1)}, f32[16,16,128]{2,1,0:T(8,128)}, u32[]{:S(2)}) copy-start(f32[16,16,128]{2,1,0:T(8,128)} %get-tuple-element.8) | copy-start | bytes 393220

commit v2 on v1

--- a/solution.py
+++ b/solution.py
@@ -248,30 +248,54 @@
     )(block)
 
 
-def all_reduce(arrays, collective_id):
+def tile_of(width, limit):
+    return max([t for t in range(128, limit + 1, 128) if width % t == 0], default=width)
+
+
+def cross_sums(kernel_rows, rows_t, small, collective_id):
     n = lax.axis_size("row")
     grid = Grid(n)
-    parts = [(i, *p) for i, a in enumerate(arrays) for p in parts_of(a.shape[2])]
-    parts.sort(key=lambda p: -p[0])
+    height, total = kernel_rows.shape
+    block = rows_t.shape[0] // n
+    shapes = [(n, block, total), small.shape]
+    parts = [(i, *p) for i, shape in enumerate(shapes) for p in parts_of(shape[2])]
+    parts.sort(key=lambda p: (-p[0], p[3][0] == "z", p[1]))
     orders = [p[3] for p in parts]
     numbered = list(enumerate(orders))
-    count = len(arrays)
-
-    def kernel(*refs):
-        sources, outs, held = refs[:count], refs[count : 2 * count], refs[2 * count : 3 * count]
-        inbox, load_sem, keep_sem, sum_send, sum_recv, send, recv = refs[3 * count :]
+
+    def body(
+        kernel_ref,
+        rows_ref,
+        small_ref,
+        out,
+        small_out,
+        held_big,
+        held_small,
+        kernel_held,
+        inbox,
+        load_sem,
+        small_sem,
+        keep_sem,
+        sum_send,
+        sum_recv,
+        send,
+        recv,
+    ):
+        held, outs = (held_big, held_small), (out, small_out)
         grid.locate()
 
-        def load(i, row):
-            return pltpu.make_async_copy(sources[i].at[row], held[i].at[row], load_sem.at[i, row])
-
-        for rel in reversed(grid.rels):
-            for i in range(count):
-
-                @when([grid.valid(rel)])
-                def _(rel=rel, i=i):
-                    load(i, grid.index(rel)).start()
-
+        def load(part):
+            _, start, width, _ = parts[part]
+            columns = pl.ds(start, width)
+            return pltpu.make_async_copy(
+                kernel_ref.at[:, columns], kernel_held.at[:, columns], load_sem.at[part]
+            )
+
+        load_small = pltpu.make_async_copy(small_ref, held_small, small_sem)
+        load_small.start()
+        for part, (i, _, _, _) in enumerate(parts):
+            if i == 0:
+                load(part).start()
         grid.barrier()
 
         def kept(part, row):
@@ -296,16 +320,40 @@
                 device_id_type=MESH,
             )
 
+        def pass_on(rel, part, order):
+            @when([grid.valid(rel)])
+            def _():
+                sum_copy(rel, part, order).start()
+
+        for part, order in numbered:
+            i, start, width, _ = parts[part]
+            if i == 0:
+                load(part).wait()
+                tile = tile_of(width, 1280)
+
+                @pl.loop(0, width // tile)
+                def _(step, start=start, tile=tile):
+                    columns = pl.ds(pl.multiple_of(start + step * tile, 128), tile)
+                    product = jnp.dot(
+                        rows_ref[...],
+                        kernel_held[:, columns],
+                        precision=lax.Precision.HIGHEST,
+                        preferred_element_type=jnp.float32,
+                    )
+                    for row in range(n):
+                        held_big[row, :, columns] = product[row * block : (row + 1) * block]
+
+            else:
+                load_small.wait()
+            for rel in reversed(grid.rels[1:]):
+                if not grid.away(order, rel):
+                    pass_on(rel, part, order)
+
         for rel in reversed(grid.rels):
-            for i in range(count):
-
-                @when([grid.valid(rel)])
-                def _(rel=rel, i=i):
-                    load(i, grid.index(rel)).wait()
-
             for part, order in numbered:
                 i, start, width, _ = parts[part]
-                for link in grid.away(order, rel):
+                links = grid.away(order, rel)
+                for link in links:
 
                     @when([grid.valid(rel), grid.has(link)])
                     def _(rel=rel, part=part, order=order, link=link):
@@ -317,11 +365,8 @@
                         held[i][row, :, columns] = held[i][row, :, columns] + inbox[part][here][at]
 
                 if rel != (0, 0, 0):
-
-                    @when([grid.valid(rel)])
-                    def _(rel=rel, part=part, order=order):
-                        sum_copy(rel, part, order).start()
-
+                    if links:
+                        pass_on(rel, part, order)
                 else:
                     pltpu.make_async_copy(
                         kept(part, grid.me), dst(part, grid.me), keep_sem.at[part]
@@ -351,20 +396,26 @@
                     ).wait()
 
     return pl.pallas_call(
-        kernel,
-        out_shape=[jax.ShapeDtypeStruct(a.shape, a.dtype) for a in arrays],
-        in_specs=[pl.BlockSpec(memory_space=pl.ANY)] * count,
-        out_specs=[pl.BlockSpec(memory_space=pl.ANY)] * count,
+        body,
+        out_shape=[jax.ShapeDtypeStruct(shape, jnp.float32) for shape in shapes],
+        in_specs=[
+            pl.BlockSpec(memory_space=pl.ANY),
+            pl.BlockSpec(memory_space=pltpu.VMEM),
+            pl.BlockSpec(memory_space=pl.ANY),
+        ],
+        out_specs=[pl.BlockSpec(memory_space=pl.ANY)] * 2,
         scratch_shapes=[
-            *[pltpu.VMEM(a.shape, a.dtype) for a in arrays],
+            *[pltpu.VMEM(shape, jnp.float32) for shape in shapes],
+            pltpu.VMEM((height, total), jnp.float32),
             [
                 [
-                    pltpu.VMEM((grid.slots(order, link), arrays[i].shape[1], width), jnp.float32)
+                    pltpu.VMEM((grid.slots(order, link), shapes[i][1], width), jnp.float32)
                     for link in grid.links()
                 ]
                 for i, _, width, order in parts
             ],
-            pltpu.SemaphoreType.DMA((count, n)),
+            pltpu.SemaphoreType.DMA((len(parts),)),
+            pltpu.SemaphoreType.DMA,
             pltpu.SemaphoreType.DMA((len(parts),)),
             pltpu.SemaphoreType.DMA((len(parts), n)),
             sem_shapes(grid, orders),
@@ -374,42 +425,85 @@
         compiler_params=pltpu.CompilerParams(
             collective_id=collective_id, has_side_effects=True, vmem_limit_bytes=60 * 2**20
         ),
-    )(*arrays)
+    )(kernel_rows, rows_t, small)
+
+
+def deflate(kernel_rows, sums, rows, own):
+    height, total = kernel_rows.shape
+    comp = sums.shape[0]
+    tile = tile_of(total, 2048)
+
+    def body(kernel_ref, sums_ref, rows_ref, own_ref, deflated_ref, own_out):
+        def times(left):
+            return jnp.dot(
+                left[...],
+                sums_ref[...],
+                precision=lax.Precision.HIGHEST,
+                preferred_element_type=jnp.float32,
+            )
+
+        deflated_ref[...] = kernel_ref[...] - times(rows_ref)
+        own_out[...] = times(own_ref)
+
+    def columns(size):
+        return pl.BlockSpec((size, tile), lambda i: (0, i))
+
+    return pl.pallas_call(
+        body,
+        grid=(total // tile,),
+        out_shape=[
+            jax.ShapeDtypeStruct(kernel_rows.shape, jnp.float32),
+            jax.ShapeDtypeStruct((own.shape[0], total), jnp.float32),
+        ],
+        in_specs=[
+            columns(height),
+            columns(comp),
+            pl.BlockSpec(rows.shape, lambda i: (0, 0)),
+            pl.BlockSpec(own.shape, lambda i: (0, 0)),
+        ],
+        out_specs=[columns(height), columns(own.shape[0])],
+    )(kernel_rows, sums, rows, own)
 
 
 def local(kernel, basis, responses):
     highest = lax.Precision.HIGHEST
     n = lax.axis_size("row")
-    row_count = kernel.shape[0] * n
-    resp_count = responses.shape[1] * lax.axis_size("col")
+    height, total = kernel.shape
+    responses_here = responses.shape[1]
+    row_count = height * n
+    resp_count = responses_here * lax.axis_size("col")
     comp = basis.shape[1] * n
     root_rows = math.sqrt(row_count)
     last_dims = (((1,), (1,)), ((), ()))
     first_dims = (((0,), (0,)), ((), ()))
 
-    all_basis = all_gather(basis.T, 0).reshape(comp, basis.shape[0])
+    all_basis = all_gather(basis.T, 0).reshape(comp, total)
     partial_proj = lax.dot_general(kernel, all_basis, last_dims, precision=highest)
     projected = lax.psum(partial_proj, "col")
-    all_projected = all_gather(projected, 1).reshape(row_count, comp)
-    gram_mat = lax.dot_general(all_projected, all_projected, first_dims, precision=highest)
-    factor = jnp.linalg.cholesky(gram_mat / row_count)
-    scores = jax.scipy.linalg.solve_triangular(factor, projected.T, lower=True).T
-
-    load_part = lax.dot_general(scores, kernel, first_dims, precision=highest) / root_rows
-    weight_part = lax.dot_general(responses, scores, first_dims, precision=highest) / root_rows
-    all_loadings, all_weights = all_reduce(
-        [
-            load_part.reshape(n, comp // n, kernel.shape[1]),
-            weight_part.reshape(n, responses.shape[1] // n, comp),
-        ],
-        2,
+
+    small_part = lax.dot_general(
+        jnp.concatenate([responses, projected], axis=1), projected, first_dims, precision=highest
     )
-    loadings = lax.dynamic_index_in_dim(all_loadings, lax.axis_index("row"), keepdims=False)
-    weights = all_weights.reshape(responses.shape[1], comp)
+    sums, small = cross_sums(
+        kernel, projected.T, small_part.reshape(n, (responses_here + comp) // n, comp), 1
+    )
+    small = small.reshape(responses_here + comp, comp)
+    factor = jnp.linalg.cholesky(small[responses_here:] / row_count)
+    right = jnp.concatenate(
+        [projected.T, small[:responses_here].T, jnp.eye(comp, dtype=jnp.float32)], axis=1
+    )
+    solved = jax.scipy.linalg.solve_triangular(factor, right, lower=True)
+    scores = solved[:, :height].T
+    weights = solved[:, height : height + responses_here].T / root_rows
+    inverse = solved[:, height + responses_here :] / root_rows
     next_part = jnp.dot(responses, weights, precision=highest) / math.sqrt(resp_count)
     basis_next = lax.psum(next_part, "col")
-    all_loadings = all_loadings.reshape(comp, kernel.shape[1])
-    deflated = kernel - jnp.dot(scores, all_loadings, precision=highest) / root_rows
+    deflated, loadings = deflate(
+        kernel,
+        sums.reshape(comp, total),
+        jnp.dot(scores, inverse, precision=highest) / root_rows,
+        lax.dynamic_slice_in_dim(inverse, lax.axis_index("row") * (comp // n), comp // n),
+    )
     return (scores, loadings, weights, deflated, basis_next)
 
 

time: 476 us -> 487 us (1.023)
  Pallas kernels: 380 us -> 432 us
  matrix products: 60 us -> 19.6 us
    pallas_call x1 -> x2, Pallas kernels: 239 us -> 308 us  [the longest x1 287 us: cross_sums(): pl.pallas_call(body, out_shape=[jax.ShapeDtypeStruct(shape, jnp.float32)...]
    dot_general x4 -> x2, matrix products: 37.5 us -> 1.97 us  [the longest x1 1.17 us: local(): lax.dot_general(jnp.concatenate([responses, projected], axis=1), projecte...]
    pallas_call x2 -> x1, Pallas kernels: 142 us -> 123 us  [all_gather(): pl.pallas_call(kernel, out_shape=jax.ShapeDtypeStruct((n, *block.shape),...]
where the time goes in v2:
time: 487 us
  Pallas kernels  432 us (89%)
  other arithmetic  23.6 us (5%)
  matrix products  19.6 us (4%)
  blocking collectives  7.58 us (2%)
    pallas_call x1, Pallas kernels, cross_sums(): pl.pallas_call(body, out_shape=[jax.ShapeDtypeStruct(shape, jnp.float32)...  287 us
    pallas_call x1, Pallas kernels, all_gather(): pl.pallas_call(kernel, out_shape=jax.ShapeDtypeStruct((n, *block.shape),...  123 us
    pallas_call x1, Pallas kernels, deflate(): pl.pallas_call(body, grid=(total // tile,), out_shape=[jax.ShapeDtypeStru...  21.4 us
    dot_general x1, matrix products, local(): lax.dot_general(kernel, all_basis, last_dims, precision=highest)  17.1 us
    another operation x3, other arithmetic, local(): factor = jnp.linalg.cholesky(small[responses_here:] / row_count)  12.4 us
    another operation x2, other arithmetic, local(): solved = jax.scipy.linalg.solve_triangular(factor, right, lower=True)  10.5 us

profile of v2, /device:TPU:0, one launch (start us, length us, event | category | flops | bytes accessed | tf_op | source)
XLA Modules:
  0.0 486.6 jit_solution(15322747202388841574)
XLA Ops:
  0.7 0.1 copy.18
  0.7 123.2 %shard_map.74 = f32[16,8,32768]{2,1,0:T(8,128)} custom-call(f32[8,32768]{1,0:T(8,128)} %bitcast.31), custom_call_target="tpu_custom_call" | custom-call | tf_op jit(solution)/shard_map/pallas_call | solution.py:237
  123.9 0.0 copy-start.1
  123.9 17.1 %fusion = f32[64,128]{0,1:T(8,128)S(1)} fusion(f32[64,32768]{1,0:T(8,128)} %kernel_ref.3, f32[16,8,32768]{2,1,0:T(8,128)} %shard_map.74), kind=kOutput, calls=%fused_computation | convolution fusion | flops 3221225472 | bytes 25198592 | tf_op jit(solution)/shard_map/dot_general | solution.py:481
  141.0 3.6 psum.14
  144.6 0.0 copy-start
  144.6 0.1 copy.17
  144.7 0.1 copy.14
  144.8 0.0 copy-done.1
  144.8 1.2 fusion.10
  146.0 0.0 copy-done
  146.0 287.1 %shard_map.75 = (f32[16,8,32768]{2,1,0:T(8,128)}, f32[16,24,128]{2,1,0:T(8,128)}) custom-call(f32[64,32768]{1,0:T(8,128)} %kernel_ref.3, f32[128,64]{1,0:T(8,128)} %bitcast.30, f32[16,24,128]{2,1,0:T(8,128)} %bitcast.32), custom_call_target="tpu_custom_call" | custom-call | tf_op jit(solution)/shard_map/pallas_call | solution.py:398
  433.1 0.8 slice.32
  433.9 0.9 slice_bitcast_fusion
  434.8 0.1 copy.21
  435.0 0.1 copy.16
  435.1 11.7 %cholesky.17 = f32[128,128]{1,0:T(8,128)S(1)} custom-call(f32[128,128]{1,0:T(8,128)S(1)} %fusion.16), custom_call_target="Cholesky" | custom-call | tf_op jit(solution)/shard_map/jit(cholesky)/cholesky | solution.py:491
  446.8 0.6 compare_reduce_fusion
  447.5 0.7 fusion.14
  448.1 9.8 %custom-call.7 = f32[1,128,128]{1,2,0:T(8,128)S(1)} custom-call(f32[1,128,128]{2,1,0:T(8,128)S(1)} %fusion.14), custom_call_target="InvertDiagBlocksLowerTriangular" | custom-call | tf_op jit(solution)/shard_map/jit(_solve_triangular)/triangular_solve | solution.py:495
  457.9 0.3 fusion.3
  458.3 0.2 fusion.2
  458.5 4.0 psum.15
  462.5 0.6 slice_bitcast_fusion.1
  463.1 0.1 copy.22
  463.2 0.8 convolution_multiply_fusion.1.rows_ref
  464.0 0.7 fusion.9
  464.7 0.6 constant_dynamic-slice_fusion.own_ref
  465.3 21.4 %shard_map.76 = (f32[64,32768]{1,0:T(8,128)}, f32[8,32768]{1,0:T(8,128)}) custom-call(f32[64,32768]{1,0:T(8,128)} %kernel_ref.3, f32[128,32768]{1,0:T(8,128)} %bitcast.28, f32[64,128]{1,0:T(8,128)} %convolution_multiply_fusion.1.rows_ref, f32[8,128]{1,0:T(8,128)} %constant_dynamic-slice_fusion.own_ref), custom_call_target="tpu_custom_call" | custom-call | tf_op jit(solution)/shard_map/pallas_call | solution.py:451
  (6 shorter events, 0.1 us)
Async XLA Ops:
  123.9 20.9 %copy-start.1 = (f32[64,256]{1,0:T(8,128)S(1)}, f32[64,256]{1,0:T(8,128)}, u32[]{:S(2)}) copy-start(f32[64,256]{1,0:T(8,128)} %param.5) | copy-start | bytes 196612
  144.6 1.4 copy-start

commit v3 on v1

--- a/solution.py
+++ b/solution.py
@@ -246,6 +246,10 @@
         ],
         compiler_params=pltpu.CompilerParams(collective_id=collective_id, has_side_effects=True),
     )(block)
+
+
+def tile_of(width, limit):
+    return max([t for t in range(128, limit + 1, 128) if width % t == 0], default=width)
 
 
 def all_reduce(arrays, collective_id):
@@ -377,39 +381,87 @@
     )(*arrays)
 
 
+def deflate(kernel_rows, sums, rows, own):
+    height, total = kernel_rows.shape
+    comp = sums.shape[0]
+    tile = tile_of(total, 2048)
+
+    def body(kernel_ref, sums_ref, rows_ref, own_ref, deflated_ref, own_out):
+        def times(left):
+            return jnp.dot(
+                left[...],
+                sums_ref[...],
+                precision=lax.Precision.HIGHEST,
+                preferred_element_type=jnp.float32,
+            )
+
+        deflated_ref[...] = kernel_ref[...] - times(rows_ref)
+        own_out[...] = times(own_ref)
+
+    def columns(size):
+        return pl.BlockSpec((size, tile), lambda i: (0, i))
+
+    return pl.pallas_call(
+        body,
+        grid=(total // tile,),
+        out_shape=[
+            jax.ShapeDtypeStruct(kernel_rows.shape, jnp.float32),
+            jax.ShapeDtypeStruct((own.shape[0], total), jnp.float32),
+        ],
+        in_specs=[
+            columns(height),
+            columns(comp),
+            pl.BlockSpec(rows.shape, lambda i: (0, 0)),
+            pl.BlockSpec(own.shape, lambda i: (0, 0)),
+        ],
+        out_specs=[columns(height), columns(own.shape[0])],
+    )(kernel_rows, sums, rows, own)
+
+
 def local(kernel, basis, responses):
     highest = lax.Precision.HIGHEST
     n = lax.axis_size("row")
-    row_count = kernel.shape[0] * n
-    resp_count = responses.shape[1] * lax.axis_size("col")
+    height, total = kernel.shape
+    responses_here = responses.shape[1]
+    row_count = height * n
+    resp_count = responses_here * lax.axis_size("col")
     comp = basis.shape[1] * n
     root_rows = math.sqrt(row_count)
     last_dims = (((1,), (1,)), ((), ()))
     first_dims = (((0,), (0,)), ((), ()))
 
-    all_basis = all_gather(basis.T, 0).reshape(comp, basis.shape[0])
+    all_basis = all_gather(basis.T, 0).reshape(comp, total)
     partial_proj = lax.dot_general(kernel, all_basis, last_dims, precision=highest)
     projected = lax.psum(partial_proj, "col")
-    all_projected = all_gather(projected, 1).reshape(row_count, comp)
-    gram_mat = lax.dot_general(all_projected, all_projected, first_dims, precision=highest)
-    factor = jnp.linalg.cholesky(gram_mat / row_count)
-    scores = jax.scipy.linalg.solve_triangular(factor, projected.T, lower=True).T
-
-    load_part = lax.dot_general(scores, kernel, first_dims, precision=highest) / root_rows
-    weight_part = lax.dot_general(responses, scores, first_dims, precision=highest) / root_rows
-    all_loadings, all_weights = all_reduce(
+
+    small_part = lax.dot_general(
+        jnp.concatenate([responses, projected], axis=1), projected, first_dims, precision=highest
+    )
+    sums_part = lax.dot_general(projected, kernel, first_dims, precision=highest)
+    sums, small = all_reduce(
         [
-            load_part.reshape(n, comp // n, kernel.shape[1]),
-            weight_part.reshape(n, responses.shape[1] // n, comp),
+            sums_part.reshape(n, comp // n, total),
+            small_part.reshape(n, (responses_here + comp) // n, comp),
         ],
-        2,
-    )
-    loadings = lax.dynamic_index_in_dim(all_loadings, lax.axis_index("row"), keepdims=False)
-    weights = all_weights.reshape(responses.shape[1], comp)
+        1,
+    )
+    small = small.reshape(responses_here + comp, comp)
+    factor = jnp.linalg.cholesky(small[responses_here:] / row_count)
+    right = jnp.concatenate(
+        [projected.T, small[:responses_here].T, jnp.eye(comp, dtype=jnp.float32)], axis=1
+    )
+    solved = jax.scipy.linalg.solve_triangular(factor, right, lower=True)
+    scores = solved[:, :height].T
+    weights = solved[:, height : height + responses_here].T / root_rows
+    inverse = solved[:, height + responses_here :] / root_rows
     next_part = jnp.dot(responses, weights, precision=highest) / math.sqrt(resp_count)
     basis_next = lax.psum(next_part, "col")
-    all_loadings = all_loadings.reshape(comp, kernel.shape[1])
-    deflated = kernel - jnp.dot(scores, all_loadings, precision=highest) / root_rows
+    deflated, loadings = deflate(
+        kernel,
+        sums.reshape(comp, total),
+        jnp.dot(scores, inverse, precision=highest) / root_rows,
+        lax.dynamic_slice_in_dim(inverse, lax.axis_index("row") * (comp // n), comp // n),
+    )
     return (scores, loadings, weights, deflated, basis_next)
 
 

time: 476 us -> 466 us (0.979)
  matrix products: 60 us -> 41.9 us
  Pallas kernels: 380 us -> 388 us
    pallas_call x0 -> x1, Pallas kernels: none -> 21.4 us  [deflate(): pl.pallas_call(body, grid=(total // tile,), out_shape=[jax.ShapeDtypeStru...]
    pallas_call x2 -> x1, Pallas kernels: 142 us -> 123 us  [all_gather(): pl.pallas_call(kernel, out_shape=jax.ShapeDtypeStruct((n, *block.shape),...]
    dot_general x4 -> x3, matrix products: 37.5 us -> 20 us  [the longest x1 18 us: local(): lax.dot_general(projected, kernel, first_dims, precision=highest)]
    pallas_call x1, Pallas kernels: 239 us -> 244 us  [all_reduce(): pl.pallas_call(kernel, out_shape=[jax.ShapeDtypeStruct(a.shape, a.dtype)...]
where the time goes in v3:
time: 466 us; the launch traced here: 465 us
  Pallas kernels  388 us (83%)
  matrix products  41.9 us (9%)
  other arithmetic  23.6 us (5%)
  blocking collectives  7.4 us (2%)
    pallas_call x1, Pallas kernels, all_reduce(): pl.pallas_call(kernel, out_shape=[jax.ShapeDtypeStruct(a.shape, a.dtype)...  244 us
    pallas_call x1, Pallas kernels, all_gather(): pl.pallas_call(kernel, out_shape=jax.ShapeDtypeStruct((n, *block.shape),...  123 us
    pallas_call x1, Pallas kernels, deflate(): pl.pallas_call(body, grid=(total // tile,), out_shape=[jax.ShapeDtypeStru...  21.4 us
    dot_general x1, matrix products, local(): lax.dot_general(kernel, all_basis, last_dims, precision=highest)  21.3 us
    dot_general x1, matrix products, local(): lax.dot_general(projected, kernel, first_dims, precision=highest)  18 us
    another operation x3, other arithmetic, local(): factor = jnp.linalg.cholesky(small[responses_here:] / row_count)  12.4 us
    another operation x2, other arithmetic, local(): solved = jax.scipy.linalg.solve_triangular(factor, right, lower=True)  10.5 us

profile of v3, /device:TPU:0, one launch (start us, length us, event | category | flops | bytes accessed | tf_op | source)
XLA Modules:
  0.0 465.2 jit_solution(8450894403802085178)
XLA Ops:
  0.6 123.2 %shard_map.74 = f32[16,8,32768]{2,1,0:T(8,128)} custom-call(f32[8,32768]{1,0:T(8,128)} %bitcast.33), custom_call_target="tpu_custom_call" | custom-call | tf_op jit(solution)/shard_map/pallas_call | solution.py:237
  123.8 21.3 %fusion = f32[64,128]{1,0:T(8,128)S(1)} fusion(f32[64,32768]{1,0:T(8,128)} %kernel_ref.1, f32[16,8,32768]{2,1,0:T(8,128)} %shard_map.74), kind=kOutput, calls=%fused_computation.1 | convolution fusion | flops 3221225472 | bytes 25198592 | tf_op jit(solution)/shard_map/dot_general | solution.py:434
  145.1 3.4 psum.14
  148.5 0.0 copy-start
  148.6 18.0 %convolution_bitcast_fusion.refs_0_ = f32[16,8,32768]{2,1,0:T(8,128)} fusion(f32[64,128]{1,0:T(8,128)S(1)} %psum.14, f32[64,32768]{1,0:T(8,128)} %kernel_ref.1), kind=kOutput, calls=%fused_computation | convolution fusion | flops 3221225472 | bytes 25198592 | tf_op jit(solution)/shard_map/dot_general | solution.py:440
  166.6 0.0 copy-done
  166.6 1.2 fusion.10
  167.8 243.7 %shard_map.75 = (f32[16,8,32768]{2,1,0:T(8,128)}, f32[16,24,128]{2,1,0:T(8,128)}) custom-call(f32[16,8,32768]{2,1,0:T(8,128)} %convolution_bitcast_fusion.refs_0_, f32[16,24,128]{2,1,0:T(8,128)} %bitcast.34), custom_call_target="tpu_custom_call" | custom-call | tf_op jit(solution)/shard_map/pallas_call | solution.py:357
  411.5 0.8 slice.32
  412.3 0.1 copy.17
  412.4 0.1 copy.14
  412.5 11.7 %cholesky.17 = f32[128,128]{1,0:T(8,128)S(1)} custom-call(f32[128,128]{1,0:T(8,128)S(1)} %fusion.16), custom_call_target="Cholesky" | custom-call | tf_op jit(solution)/shard_map/jit(cholesky)/cholesky | solution.py:449
  424.3 0.6 compare_reduce_fusion
  424.9 0.7 fusion.14
  425.6 9.8 %custom-call.7 = f32[1,128,128]{1,2,0:T(8,128)S(1)} custom-call(f32[1,128,128]{2,1,0:T(8,128)S(1)} %fusion.14), custom_call_target="InvertDiagBlocksLowerTriangular" | custom-call | tf_op jit(solution)/shard_map/jit(_solve_triangular)/triangular_solve | solution.py:453
  435.4 0.9 slice_bitcast_fusion
  436.3 0.1 copy.15
  436.4 0.3 fusion.3
  436.8 0.1 copy.18
  436.9 0.8 convolution_multiply_fusion.1.rows_ref
  437.7 0.6 constant_dynamic-slice_fusion.own_ref
  438.3 21.4 %shard_map.76 = (f32[64,32768]{1,0:T(8,128)}, f32[8,32768]{1,0:T(8,128)}) custom-call(f32[64,32768]{1,0:T(8,128)} %kernel_ref.1, f32[128,32768]{1,0:T(8,128)} %bitcast.32, f32[64,128]{1,0:T(8,128)} %convolution_multiply_fusion.1.rows_ref, f32[8,128]{1,0:T(8,128)} %constant_dynamic-slice_fusion.own_ref), custom_call_target="tpu_custom_call" | custom-call | tf_op jit(solution)/shard_map/pallas_call | solution.py:404
  459.7 0.7 fusion.9
  460.3 0.2 fusion.2
  460.5 4.0 psum.15
  464.5 0.6 slice_bitcast_fusion.1
  (6 shorter events, 0.1 us)
Async XLA Ops:
  148.5 18.0 %copy-start = (f32[64,256]{1,0:T(8,128)S(1)}, f32[64,256]{1,0:T(8,128)}, u32[]{:S(2)}) copy-start(f32[64,256]{1,0:T(8,128)} %param.5) | copy-start | bytes 196612

commit v4 on v3

--- a/solution.py
+++ b/solution.py
@@ -387,16 +387,15 @@
     tile = tile_of(total, 2048)
 
     def body(kernel_ref, sums_ref, rows_ref, own_ref, deflated_ref, own_out):
-        def times(left):
-            return jnp.dot(
-                left[...],
-                sums_ref[...],
-                precision=lax.Precision.HIGHEST,
-                preferred_element_type=jnp.float32,
-            )
-
-        deflated_ref[...] = kernel_ref[...] - times(rows_ref)
-        own_out[...] = times(own_ref)
+        both = jnp.concatenate([rows_ref[...], own_ref[...]], axis=0)
+        product = jnp.dot(
+            both,
+            sums_ref[...],
+            precision=lax.Precision.HIGHEST,
+            preferred_element_type=jnp.float32,
+        )
+        deflated_ref[...] = kernel_ref[...] - product[:height]
+        own_out[...] = product[height:]
 
     def columns(size):
         return pl.BlockSpec((size, tile), lambda i: (0, i))

time: 466 us -> 464 us (level)
  no operation moved by 1% of the time
where the time goes in v4:
time: 464 us
  Pallas kernels  387 us (83%)
  matrix products  41.9 us (9%)
  other arithmetic  23.6 us (5%)
  blocking collectives  7.4 us (2%)
    pallas_call x1, Pallas kernels, all_reduce(): pl.pallas_call(kernel, out_shape=[jax.ShapeDtypeStruct(a.shape, a.dtype)...  244 us
    pallas_call x1, Pallas kernels, all_gather(): pl.pallas_call(kernel, out_shape=jax.ShapeDtypeStruct((n, *block.shape),...  123 us
    dot_general x1, matrix products, local(): lax.dot_general(kernel, all_basis, last_dims, precision=highest)  21.3 us
    pallas_call x1, Pallas kernels, deflate(): pl.pallas_call(body, grid=(total // tile,), out_shape=[jax.ShapeDtypeStru...  20 us
    dot_general x1, matrix products, local(): lax.dot_general(projected, kernel, first_dims, precision=highest)  18 us
    another operation x3, other arithmetic, local(): factor = jnp.linalg.cholesky(small[responses_here:] / row_count)  12.4 us
    another operation x2, other arithmetic, local(): solved = jax.scipy.linalg.solve_triangular(factor, right, lower=True)  10.5 us

profile of v4, /device:TPU:0, one launch (start us, length us, event | category | flops | bytes accessed | tf_op | source)
XLA Modules:
  0.0 463.8 jit_solution(12868041134323185547)
XLA Ops:
  0.6 123.2 %shard_map.74 = f32[16,8,32768]{2,1,0:T(8,128)} custom-call(f32[8,32768]{1,0:T(8,128)} %bitcast.33), custom_call_target="tpu_custom_call" | custom-call | tf_op jit(solution)/shard_map/pallas_call | solution.py:237
  123.8 21.3 %fusion = f32[64,128]{1,0:T(8,128)S(1)} fusion(f32[64,32768]{1,0:T(8,128)} %kernel_ref.1, f32[16,8,32768]{2,1,0:T(8,128)} %shard_map.74), kind=kOutput, calls=%fused_computation.1 | convolution fusion | flops 3221225472 | bytes 25198592 | tf_op jit(solution)/shard_map/dot_general | solution.py:433
  145.1 3.4 psum.14
  148.5 0.0 copy-start
  148.6 18.0 %convolution_bitcast_fusion.refs_0_ = f32[16,8,32768]{2,1,0:T(8,128)} fusion(f32[64,128]{1,0:T(8,128)S(1)} %psum.14, f32[64,32768]{1,0:T(8,128)} %kernel_ref.1), kind=kOutput, calls=%fused_computation | convolution fusion | flops 3221225472 | bytes 25198592 | tf_op jit(solution)/shard_map/dot_general | solution.py:439
  166.6 0.0 copy-done
  166.6 1.2 fusion.10
  167.8 243.7 %shard_map.75 = (f32[16,8,32768]{2,1,0:T(8,128)}, f32[16,24,128]{2,1,0:T(8,128)}) custom-call(f32[16,8,32768]{2,1,0:T(8,128)} %convolution_bitcast_fusion.refs_0_, f32[16,24,128]{2,1,0:T(8,128)} %bitcast.34), custom_call_target="tpu_custom_call" | custom-call | tf_op jit(solution)/shard_map/pallas_call | solution.py:357
  411.5 0.8 slice.32
  412.3 0.1 copy.17
  412.4 0.1 copy.14
  412.5 11.7 %cholesky.17 = f32[128,128]{1,0:T(8,128)S(1)} custom-call(f32[128,128]{1,0:T(8,128)S(1)} %fusion.16), custom_call_target="Cholesky" | custom-call | tf_op jit(solution)/shard_map/jit(cholesky)/cholesky | solution.py:448
  424.3 0.6 compare_reduce_fusion
  424.9 0.7 fusion.14
  425.6 9.8 %custom-call.7 = f32[1,128,128]{1,2,0:T(8,128)S(1)} custom-call(f32[1,128,128]{2,1,0:T(8,128)S(1)} %fusion.14), custom_call_target="InvertDiagBlocksLowerTriangular" | custom-call | tf_op jit(solution)/shard_map/jit(_solve_triangular)/triangular_solve | solution.py:452
  435.4 0.9 slice_bitcast_fusion
  436.3 0.1 copy.15
  436.4 0.3 fusion.3
  436.8 0.1 copy.18
  436.9 0.8 convolution_multiply_fusion.1.rows_ref
  437.7 0.6 constant_dynamic-slice_fusion.own_ref
  438.3 20.0 %shard_map.76 = (f32[64,32768]{1,0:T(8,128)}, f32[8,32768]{1,0:T(8,128)}) custom-call(f32[64,32768]{1,0:T(8,128)} %kernel_ref.1, f32[128,32768]{1,0:T(8,128)} %bitcast.32, f32[64,128]{1,0:T(8,128)} %convolution_multiply_fusion.1.rows_ref, f32[8,128]{1,0:T(8,128)} %constant_dynamic-slice_fusion.own_ref), custom_call_target="tpu_custom_call" | custom-call | tf_op jit(solution)/shard_map/pallas_call | solution.py:403
  458.3 0.7 fusion.9
  458.9 0.2 fusion.2
  459.2 4.0 psum.15
  463.2 0.6 slice_bitcast_fusion.1
  (6 shorter events, 0.1 us)
Async XLA Ops:
  148.5 18.0 %copy-start = (f32[64,256]{1,0:T(8,128)S(1)}, f32[64,256]{1,0:T(8,128)}, u32[]{:S(2)}) copy-start(f32[64,256]{1,0:T(8,128)} %param.5) | copy-start | bytes 196612
